TPU v7x, 32 devices: a whole 2x2x4 slice. The times are simulated.
32 devices in a mesh: macro: 16 (over z, x, core), vox: 2 (over y).
Axes of the slice: x: 2, y: 2, z: 4, core: 2. Of those that a mesh axis runs over, the one named last changes fastest.
Arguments:
- displacement: float32 [3, 1024], P(None, 'macro'), may hold values from -1.2 to 1.2
- load: float32 [3, 1024], P(None, 'macro'), may hold values from -6 to 6
- conn: int32 [8, 1024], P(None, 'macro'), may hold values from 0 to 79
- halo_list: int32 [256], P('macro'), may hold values from 0 to 63
- grad_ops: float32 [3, 8, 1024], P(None, None, 'macro'), may hold values from -3 to 3
- volume: float32 [1024], P('macro'), may hold values from 0.5 to 2
- elastic_moduli: float32 [2, 1024], P(None, 'macro'), may hold values from 1 to 4
- plastic_mask: int32 [1024], P('macro'), may hold values from 0 to 1, as said below
- new_owner: int32 [1024], P('macro'), may hold values from -1 to 15, as said below
- state: float32 [7, 1024, 16, 256], P(None, 'macro', 'vox'), may hold values from -0.6 to 1, as said below
- micro_moduli: float32 [4, 16, 256], P(None, 'vox'), may hold values from 0.5 to 6
Outputs:
- residual: float32 [3, 1024], P(None, 'macro')
- moved_state: float32 [7, 384, 16, 256], P(None, 'macro', 'vox')
Inputs may be any that keep to these rules, and one draw needn't show every extreme that they name: `plastic_mask`: each group's 64 points hold at most 48 plastic ones, 384 in all. `new_owner`: -1 exactly at elastic points; every group becomes the owner of exactly 24 plastic points, at most 3 of them from any one group. `state`: component 6 is nonnegative.
All inputs are finite; a program needn't handle non-finite values.
Results may differ from a plain program's by a relative error of at most 0.0001.
Values sent between devices are 32-bit elements; how exact they have to be, the bound alone decides.
A program may use at most 64 MiB of HBM per device.

v0:
```python
import math
import jax
import jax.numpy as jnp
from jax import lax
from jax.sharding import PartitionSpec as P

RECV_AGG = 24
PLASTIC_MAX = 48
VOX_SIDE = 16
VOX_PLANE = 256
SWEEPS = 4
LAM_REF = 3.0
MU_REF = 3.0
FULL_PREC = lax.Precision.HIGHEST


def shifted(block, axis, distance):
    devices = range(lax.axis_size(axis))
    route = [((i - distance) % len(devices), i) for i in devices]
    return lax.ppermute(block, axis, route)


def strain_tensor(disp_el, grad_el):
    products = [[jnp.sum(disp_el[i] * grad_el[j], axis=0) for j in range(3)] for i in range(3)]
    return jnp.stack(
        [
            products[0][0],
            products[1][1],
            products[2][2],
            0.5 * (products[1][2] + products[2][1]),
            0.5 * (products[0][2] + products[2][0]),
            0.5 * (products[0][1] + products[1][0]),
        ]
    )


def full_tensor(voigt):
    return [
        [voigt[0], voigt[5], voigt[4]],
        [voigt[5], voigt[1], voigt[3]],
        [voigt[4], voigt[3], voigt[2]],
    ]


def nodal_forces(stress, grad_el, volume):
    tensor = full_tensor(stress)
    return jnp.stack(
        [
            volume
            * (tensor[i][0] * grad_el[0] + tensor[i][1] * grad_el[1] + tensor[i][2] * grad_el[2])
            for i in range(3)
        ]
    )


def elastic_stress(strain, moduli):
    lame_first = moduli[0]
    shear_mod = moduli[1]
    trace = strain[0] + strain[1] + strain[2]
    return jnp.stack(
        [lame_first * trace + 2.0 * shear_mod * strain[c] for c in range(3)]
        + [2.0 * shear_mod * strain[c] for c in range(3, 6)]
    )


def return_map(strain, state, props):
    lame_first, shear_mod, yield_base, harden = (props[0], props[1], props[2], props[3])
    elastic = [strain[c] - state[c] for c in range(6)]
    trace = elastic[0] + elastic[1] + elastic[2]
    trial = [lame_first * trace + 2.0 * shear_mod * elastic[c] for c in range(3)] + [
        2.0 * shear_mod * elastic[c] for c in range(3, 6)
    ]
    pressure = (trial[0] + trial[1] + trial[2]) / 3.0
    deviator = [
        trial[0] - pressure,
        trial[1] - pressure,
        trial[2] - pressure,
        trial[3],
        trial[4],
        trial[5],
    ]
    squared = (
        deviator[0] ** 2
        + deviator[1] ** 2
        + deviator[2] ** 2
        + 2.0 * (deviator[3] ** 2 + deviator[4] ** 2 + deviator[5] ** 2)
    )
    equivalent = jnp.sqrt(1.5 * squared)
    strength = yield_base + harden * state[6]
    excess = jnp.maximum(equivalent - strength, 0.0)
    stiffer = 3.0 * shear_mod + harden
    factor = excess / (stiffer * jnp.maximum(equivalent, strength))
    stress = jnp.stack([trial[c] - 3.0 * shear_mod * factor * deviator[c] for c in range(6)])
    new_state = jnp.stack(
        [state[c] + 1.5 * factor * deviator[c] for c in range(6)] + [state[6] + excess / stiffer]
    )
    return (stress, new_state)


def green_apply(tau, freq_x, freq_y, freq_z):
    trac_x = tau[0] * freq_x + tau[5] * freq_y + tau[4] * freq_z
    trac_y = tau[5] * freq_x + tau[1] * freq_y + tau[3] * freq_z
    trac_z = tau[4] * freq_x + tau[3] * freq_y + tau[2] * freq_z
    norm_sq = freq_x * freq_x + freq_y * freq_y + freq_z * freq_z
    inverse = jnp.where(norm_sq > 0, 1.0 / jnp.maximum(norm_sq, 1.0), 0.0)
    coupling = (LAM_REF + MU_REF) / (LAM_REF + 2.0 * MU_REF)
    along = (freq_x * trac_x + freq_y * trac_y + freq_z * trac_z) * inverse
    wave_x = (trac_x - coupling * along * freq_x) * inverse / MU_REF
    wave_y = (trac_y - coupling * along * freq_y) * inverse / MU_REF
    wave_z = (trac_z - coupling * along * freq_z) * inverse / MU_REF
    return [
        freq_x * wave_x,
        freq_y * wave_y,
        freq_z * wave_z,
        0.5 * (freq_y * wave_z + freq_z * wave_y),
        0.5 * (freq_x * wave_z + freq_z * wave_x),
        0.5 * (freq_x * wave_y + freq_y * wave_x),
    ]


def dft_tables():
    line_index = jnp.arange(VOX_SIDE, dtype=jnp.int32)
    line_phase = line_index[:, None] * line_index[None, :] % VOX_SIDE
    plane_index = jnp.arange(VOX_PLANE, dtype=jnp.int32)
    plane_rows = plane_index // VOX_SIDE
    plane_cols = plane_index % VOX_SIDE
    plane_phase = (
        plane_rows[:, None] * plane_rows[None, :] + plane_cols[:, None] * plane_cols[None, :]
    ) % VOX_SIDE
    radians = 2.0 * math.pi / VOX_SIDE
    line_angle = line_phase.astype(jnp.float32) * radians
    plane_angle = plane_phase.astype(jnp.float32) * radians
    signed = jnp.where(line_index < VOX_SIDE // 2, line_index, line_index - VOX_SIDE).astype(
        jnp.float32
    )
    return (
        jnp.cos(line_angle),
        jnp.sin(line_angle),
        jnp.cos(plane_angle),
        jnp.sin(plane_angle),
        signed[:, None],
        signed[plane_rows],
        signed[plane_cols],
    )


def line_apply(table, field):
    return jnp.einsum("kx,cbxn->cbkn", table, field, precision=FULL_PREC)


def spectral_correction(stress, tables):
    cos_line, sin_line, cos_plane, sin_plane, freq_x, freq_y, freq_z = tables
    real_plane = jnp.dot(stress, cos_plane, precision=FULL_PREC)
    imag_plane = -jnp.dot(stress, sin_plane, precision=FULL_PREC)
    real_full = line_apply(cos_line, real_plane) + line_apply(sin_line, imag_plane)
    imag_full = line_apply(cos_line, imag_plane) - line_apply(sin_line, real_plane)
    green_real = jnp.stack(green_apply([real_full[c] for c in range(6)], freq_x, freq_y, freq_z))
    green_imag = jnp.stack(green_apply([imag_full[c] for c in range(6)], freq_x, freq_y, freq_z))
    back_real = line_apply(cos_line, green_real) - line_apply(sin_line, green_imag)
    back_imag = line_apply(cos_line, green_imag) + line_apply(sin_line, green_real)
    spatial = jnp.dot(back_real, cos_plane, precision=FULL_PREC) - jnp.dot(
        back_imag, sin_plane, precision=FULL_PREC
    )
    return spatial / VOX_SIDE**3


def micro_solve(states, strains, moduli_slab):
    tables = dft_tables()
    aggregates = states.shape[1]
    thickness = states.shape[2]
    ranks_vox = lax.axis_size("vox")
    per_rank = aggregates // ranks_vox
    full_moduli = lax.all_gather(moduli_slab, "vox", axis=1, tiled=True)
    gathered = lax.all_to_all(
        states.reshape(7, ranks_vox, per_rank, thickness, VOX_PLANE),
        "vox",
        split_axis=1,
        concat_axis=3,
        tiled=True,
    )
    gathered = gathered.reshape(7, per_rank, VOX_SIDE, VOX_PLANE)
    own_strain = lax.dynamic_slice_in_dim(strains, lax.axis_index("vox") * per_rank, per_rank, 1)
    strain_field = jnp.broadcast_to(own_strain[:, :, None, None], (6,) + gathered.shape[1:])
    for iteration in range(SWEEPS):
        stress, _ = return_map(strain_field, gathered, full_moduli)
        strain_field = strain_field - spectral_correction(stress, tables)
    stress, updated = return_map(strain_field, gathered, full_moduli)
    averaged = lax.all_gather(jnp.mean(stress, axis=(2, 3)), "vox", axis=1, tiled=True)
    returned = lax.all_to_all(
        updated.reshape(7, per_rank, ranks_vox, thickness, VOX_PLANE),
        "vox",
        split_axis=2,
        concat_axis=1,
        tiled=True,
    )
    return (returned.reshape(states.shape), averaged)


def pick_slots(valid, count):
    position = jnp.cumsum(valid.astype(jnp.int32)) - 1
    wanted = jnp.arange(count, dtype=jnp.int32)
    matching = (wanted[:, None] == position[None, :]) & valid[None, :]
    sources = jnp.arange(valid.shape[0], dtype=jnp.int32)
    return (jnp.sum(jnp.where(matching, sources[None, :], 0), axis=1), matching)


def local(
    displacement,
    load,
    conn,
    halo_list,
    grad_ops,
    volume,
    elastic_moduli,
    plastic_mask,
    new_owner,
    state,
    micro_moduli,
):
    groups = lax.axis_size("macro")
    own_nodes = displacement.shape[1]
    elements = conn.shape[1]
    halo_disp = shifted(displacement[:, halo_list], "macro", 1)
    local_disp = jnp.concatenate([displacement, halo_disp], axis=1)
    strain = strain_tensor(local_disp[:, conn], grad_ops)
    plastic = plastic_mask == 1
    point_ids = jnp.arange(elements, dtype=jnp.int32)
    same_owner = (
        (new_owner[:, None] == new_owner[None, :])
        & plastic[:, None]
        & plastic[None, :]
        & (point_ids[None, :] < point_ids[:, None])
    )
    owner_rank = jnp.sum(same_owner.astype(jnp.int32), axis=1)
    capacity = (PLASTIC_MAX + groups - 1) // groups
    send_slot = jnp.where(plastic, new_owner * capacity + owner_rank, -1)
    slot_ids = jnp.arange(groups * capacity, dtype=jnp.int32)
    slot_match = slot_ids[:, None] == send_slot[None, :]
    slot_valid = jnp.any(slot_match, axis=1)
    valid_float = slot_valid.astype(jnp.float32)
    slot_source = jnp.sum(jnp.where(slot_match, point_ids[None, :], 0), axis=1)
    outgoing = state[:, slot_source] * valid_float[None, :, None, None]
    strain_rows = strain[:, slot_source] * valid_float[None, :]
    received, got_strain, got_valid = (
        lax.all_to_all(outgoing, "macro", split_axis=1, concat_axis=1, tiled=True),
        lax.all_to_all(strain_rows, "macro", split_axis=1, concat_axis=1, tiled=True),
        lax.all_to_all(valid_float[None, :], "macro", split_axis=1, concat_axis=1, tiled=True),
    )
    recv_index, recv_match = pick_slots(got_valid[0] > 0.5, RECV_AGG)
    moved_state, averaged = micro_solve(
        received[:, recv_index], got_strain[:, recv_index], micro_moduli
    )
    slot_stress = jnp.dot(averaged, recv_match.astype(jnp.float32), precision=FULL_PREC)
    got_stress = lax.all_to_all(slot_stress, "macro", split_axis=1, concat_axis=1, tiled=True)
    stress_plastic = jnp.dot(got_stress, slot_match.astype(jnp.float32), precision=FULL_PREC)
    stress = jnp.where(plastic[None, :], stress_plastic, elastic_stress(strain, elastic_moduli))
    forces = nodal_forces(stress, grad_ops, volume)
    node_ids = jnp.arange(local_disp.shape[1], dtype=jnp.int32)
    node_match = (conn[:, :, None] == node_ids[None, None, :]).astype(jnp.float32)
    assembled = jnp.einsum("iae,aen->in", forces, node_match, precision=FULL_PREC)
    returned_force = shifted(assembled[:, own_nodes:], "macro", -1)
    own_ids = jnp.arange(own_nodes, dtype=jnp.int32)
    halo_match = (halo_list[:, None] == own_ids[None, :]).astype(jnp.float32)
    residual = (
        assembled[:, :own_nodes] + jnp.dot(returned_force, halo_match, precision=FULL_PREC) - load
    )
    return (residual, moved_state)


def solution(mesh):
    return jax.shard_map(
        local,
        mesh=mesh,
        in_specs=(
            P(None, "macro"),
            P(None, "macro"),
            P(None, "macro"),
            P("macro"),
            P(None, None, "macro"),
            P("macro"),
            P(None, "macro"),
            P("macro"),
            P("macro"),
            P(None, "macro", "vox", None),
            P(None, "vox", None),
        ),
        out_specs=(P(None, "macro"), P(None, "macro", "vox", None)),
        check_vma=False,
    )
```

profile of v0, /device:TPU:0, one launch (start us, length us, event | category | flops | bytes accessed | tf_op | source)
XLA Modules:
  0.0 243.6 jit_solution(13568793401414966940)
XLA Ops:
  3.7 7.4 %all-to-all-start.1 = ((f32[1,16,3]{2,0,1:T(1,128)}), f32[1,16,3]{2,0,1:T(1,128)S(1)}, u32[]{:S(2)}, u32[]{:S(2)}) async-start(f32[1,16,3]{2,0,1:T(1,128)} %bitcast.13), calls=%async_computation.1 | async-start | bytes 16384 | tf_op jit(solution)/shard_map/all_to_all | solution.py:247
  11.9 2.8 %gather_fusion.4 = f32[48,7,8,256]{3,2,1,0:T(8,128)S(1)} fusion(f32[7,64,8,256]{3,2,1,0:T(8,128)} %param.20, s32[1024]{0:T(1024)S(1)} %get-tuple-element.240), kind=kCustom, calls=%fused_computation.4 | custom fusion | bytes 5505216 | tf_op jit(solution)/shard_map/gather | solution.py:242
  14.7 1.8 multiply_bitcast_fusion
  17.5 5.2 %all-to-all-start.2 = ((f32[7,48,8,256]{3,2,0,1:T(8,128)}), f32[7,48,8,256]{3,2,0,1:T(8,128)S(1)}, u32[]{:S(2)}, u32[]{:S(2)}) async-start(f32[7,48,8,256]{3,2,0,1:T(8,128)} %multiply_bitcast_fusion), calls=%async_computation.2 | async-start | bytes 5505024 | tf_op jit(solution)/shard_map/all_to_all | solution.py:245
  25.3 4.2 %compare_select_fusion.3 = (f32[256,1]{0,1:T(1,128)S(1)}, f32[256,1]{0,1:T(1,128)S(1)}) fusion(f32[]{:T(128)} %bitcast.53, f32[]{:T(128)} %bitcast.54, f32[]{:T(128)} %bitcast.55, f32[]{:T(128)} %bitcast.56, f32[]{:T(128)} %bitcast.57, f32[]{:T(128)} %bitcast.59, f32[]{:T(128)} %bitcast.58), kind=kLoop, calls=%fused_computation.506 | loop fusion | flops 10752 | bytes 2076 | tf_op jit(solution)/shard_map/gather | solution.py:143
  29.5 5.6 %broadcast_multiply_fusion.1 = (f32[256]{0:T(256)S(1)}, f32[256]{0:T(256)S(1)}) fusion(pred[256]{0:T(512)(128)(4,1)S(1)} %compare_reduce_fusion.1, pred[256]{0:T(512)(128)(4,1)S(1)} %compare_reduce_fusion.2, pred[256]{0:T(512)(128)(4,1)S(1)} %compare_reduce_fusion.3, pred[256]{0:T(512)(128)(4,1)S(1)} %compare_reduce_fusion.4, ...), kind=kLoop, calls=%fused_computation.559 | loop fusion | flops 2560 | bytes 5412 | tf_op jit(solution)/shard_map/mul | solution.py:114
  35.2 5.6 %broadcast_multiply_fusion.2 = (f32[256]{0:T(256)S(1)}, f32[256]{0:T(256)S(1)}) fusion(pred[256]{0:T(512)(128)(4,1)S(1)} %compare_reduce_fusion.10, pred[256]{0:T(512)(128)(4,1)S(1)} %compare_reduce_fusion.11, pred[256]{0:T(512)(128)(4,1)S(1)} %compare_reduce_fusion.12, pred[256]{0:T(512)(128)(4,1)S(1)} %compare_reduce_fusion.13, ...), kind=kLoop, calls=%fused_computation.560 | loop fusion | flops 2560 | bytes 5412 | tf_op jit(solution)/shard_map/mul | solution.py:113
  40.9 31.7 %collective-permute-done = f32[3,16]{0,1:T(8,128)S(1)} collective-permute-done((f32[3,16]{0,1:T(8,128)S(1)}, f32[3,16]{0,1:T(8,128)S(1)}, u32[]{:S(2)}, u32[]{:S(2)}) %collective-permute-start) | collective-permute-done | bytes 224 | tf_op jit(solution)/shard_map/ppermute | solution.py:20
  76.2 15.5 %all-to-all-start = ((f32[6,16,3]{0,2,1:T(4,128)}), f32[6,16,3]{0,2,1:T(4,128)S(1)}, u32[]{:S(2)}, u32[]{:S(2)}) async-start(f32[6,16,3]{0,2,1:T(4,128)} %copy.230), calls=%async_computation | async-start | bytes 65536 | tf_op jit(solution)/shard_map/all_to_all | solution.py:246
  91.7 1.8 copy.236
  93.5 2.4 gather_fusion.5
  95.9 1.2 copy.238
  98.3 3.6 %all-to-all-start.3 = ((f32[7,2,12,8,256]{4,3,2,0,1:T(8,128)}), f32[7,2,12,8,256]{4,3,2,0,1:T(8,128)S(1)}, u32[]{:S(2)}, u32[]{:S(2)}) async-start(f32[7,2,12,8,256]{4,3,2,0,1:T(8,128)} %copy.238), calls=%async_computation.3 | async-start | bytes 2752512 | tf_op jit(solution)/shard_map/all_to_all | solution.py:174
  102.0 17.9 %all_gather.6 = f32[4,16,256]{2,1,0:T(8,128)S(1)} all-gather(f32[4,8,256]{2,1,0:T(8,128)S(1)} %copy-done.1), channel_id=1, replica_groups=mesh['macro'=16,'vox'=2] {'vox'}, dimensions={1}, use_global_device_ids=true | all-gather | bytes 98304 | tf_op jit(solution)/shard_map/all_gather | solution.py:173
  121.9 2.1 fusion.42
  124.1 2.1 convolution_negate_fusion.3
  126.2 1.2 fusion.204
  128.6 1.2 fusion.23
  129.8 1.2 fusion.22
  132.2 1.4 fusion.198
  134.7 1.2 fusion.20
  135.9 1.2 fusion.21
  137.1 2.1 fusion.40
  139.2 2.2 fusion.7
  142.1 2.1 fusion.38
  144.3 2.5 %convolution_negate_fusion.2 = f32[6,12,16,256]{3,2,1,0:T(8,128)S(1)} fusion(f32[6,12,16,256]{3,2,1,0:T(8,128)S(1)} %fusion.57, s32[256]{0:T(256)S(1)} %get-tuple-element.244, s32[256]{0:T(256)S(1)} %get-tuple-element.245), kind=kOutput, calls=%fused_computation.18 | convolution fusion | flops 907313152 | bytes 2361344 | tf_op jit(solution)/shard_map/dot_general | solution.py:154
  146.8 1.2 fusion.196
  148.0 1.2 fusion.192
  149.2 1.2 fusion.19
  150.3 1.2 fusion.18
  152.7 1.2 fusion.190
  153.9 1.2 fusion.194
  155.1 1.2 fusion.16
  157.4 2.3 fusion.36
  159.8 2.2 fusion.5
  162.6 2.1 fusion.34
  164.8 2.1 convolution_negate_fusion.1
  166.9 1.2 fusion.188
  168.1 1.2 fusion.184
  169.3 1.4 fusion.15
  170.7 1.2 fusion.14
  175.4 1.2 fusion.12
  177.8 2.1 fusion.32
  179.9 2.6 %fusion.3 = f32[6,12,16,256]{3,2,1,0:T(8,128)S(1)} fusion(f32[6,12,16,256]{3,2,1,0:T(8,128)S(1)} %fusion.5, f32[6,12,16,256]{3,2,1,0:T(8,128)S(1)} %fusion.32, f32[6,12,16,256]{3,2,1,0:T(8,128)S(1)} %fusion.12, s32[256]{0:T(256)S(1)} %get-tuple-element.244, s32[256]{0:T(256)S(1)} %get-tuple-element.245), kind=kOutput, calls=%fused_computation.13 | convolution fusion | flops 907902976 | bytes 4720640 | tf_op jit(solution)/shard_map/dot_general | solution.py:161
  183.2 2.1 fusion.30
  185.3 2.1 convolution_negate_fusion
  187.5 1.2 fusion.180
  188.7 1.2 fusion.176
  189.8 1.2 fusion.11
  191.0 1.2 fusion.10
  193.4 1.4 fusion.174
  194.8 1.2 fusion.178
  195.9 1.2 fusion.8
  197.1 1.2 fusion.9
  198.3 2.2 fusion.28
  200.5 2.2 fusion.1
  203.8 4.4 %all-gather = f32[2,12,6]{1,2,0:T(8,128)S(1)} all-gather(f32[1,12,6]{1,2,0:T(8,128)S(1)} %multiply_bitcast_fusion.2), channel_id=1, replica_groups=mesh['macro'=16,'vox'=2] {'vox'}, dimensions={0}, use_global_device_ids=true | all-gather | bytes 864 | tf_op jit(solution)/shard_map/all_gather | solution.py:188
  209.3 5.4 %all-to-all-start.4 = ((f32[6,16,3]{0,2,1:T(4,128)}), f32[6,16,3]{0,2,1:T(4,128)S(1)}, u32[]{:S(2)}, u32[]{:S(2)}) async-start(f32[6,16,3]{0,2,1:T(4,128)} %copy.247), calls=%async_computation.4 | async-start | bytes 65536 | tf_op jit(solution)/shard_map/all_to_all | solution.py:254
  214.8 1.2 copy.267
  216.0 5.3 %all-to-all-done.4 = f32[6,16,3]{0,2,1:T(4,128)S(1)} async-done(((f32[6,16,3]{0,2,1:T(4,128)}), f32[6,16,3]{0,2,1:T(4,128)S(1)}, u32[]{:S(2)}, u32[]{:S(2)}) %all-to-all-start.4) | async-done | bytes 1184 | tf_op jit(solution)/shard_map/all_to_all | solution.py:254
  221.4 3.6 %all-to-all-start.5 = ((f32[7,12,2,8,256]{4,3,1,0,2:T(8,128)}), f32[7,12,2,8,256]{4,3,1,0,2:T(8,128)S(1)}, u32[]{:S(2)}, u32[]{:S(2)}) async-start(f32[7,12,2,8,256]{4,3,1,0,2:T(8,128)} %copy.267), calls=%async_computation.5 | async-start | bytes 2752512 | tf_op jit(solution)/shard_map/all_to_all | solution.py:189
  225.8 1.3 collective-permute-done.1
  227.9 14.3 %all-to-all-done.5 = f32[7,12,2,8,256]{4,3,1,0,2:T(8,128)S(1)} async-done(((f32[7,12,2,8,256]{4,3,1,0,2:T(8,128)}), f32[7,12,2,8,256]{4,3,1,0,2:T(8,128)S(1)}, u32[]{:S(2)}, u32[]{:S(2)}) %all-to-all-start.5) | async-done | bytes 1376288 | tf_op jit(solution)/shard_map/all_to_all | solution.py:189
  242.2 1.2 copy.257
  (176 shorter events, 31.6 us)
Async XLA Ops:
  3.7 13.8 %all-to-all-start.1 = ((f32[1,16,3]{2,0,1:T(1,128)}), f32[1,16,3]{2,0,1:T(1,128)S(1)}, u32[]{:S(2)}, u32[]{:S(2)}) async-start(f32[1,16,3]{2,0,1:T(1,128)} %bitcast.13), calls=%async_computation.1 | async-start | bytes 16384 | tf_op jit(solution)/shard_map/all_to_all | solution.py:247
  16.5 6.2 %copy-start.4 = (f32[3,64]{1,0:T(4,128)S(1)}, f32[3,64]{1,0:T(4,128)}, u32[]{:S(2)}) copy-start(f32[3,64]{1,0:T(4,128)} %param.11) | copy-start | bytes 2308
  16.5 7.4 %copy-start.2 = (s32[8,64]{1,0:T(8,128)S(1)}, s32[8,64]{1,0:T(8,128)}, u32[]{:S(2)}) copy-start(s32[8,64]{1,0:T(8,128)} %param.13) | copy-start | bytes 6148
  16.5 57.3 %copy-start = (f32[3,8,64]{2,1,0:T(8,128)S(1)}, f32[3,8,64]{2,1,0:T(8,128)}, u32[]{:S(2)}) copy-start(f32[3,8,64]{2,1,0:T(8,128)} %param.15) | copy-start | bytes 18436
  16.5 57.4 %copy-start.3 = (f32[2,64]{1,0:T(2,128)S(1)}, f32[2,64]{1,0:T(2,128)}, u32[]{:S(2)}) copy-start(f32[2,64]{1,0:T(2,128)} %param.17) | copy-start | bytes 1540
  17.5 58.7 %all-to-all-start.2 = ((f32[7,48,8,256]{3,2,0,1:T(8,128)}), f32[7,48,8,256]{3,2,0,1:T(8,128)S(1)}, u32[]{:S(2)}, u32[]{:S(2)}) async-start(f32[7,48,8,256]{3,2,0,1:T(8,128)} %multiply_bitcast_fusion), calls=%async_computation.2 | async-start | bytes 5505024 | tf_op jit(solution)/shard_map/all_to_all | solution.py:245
  23.3 49.3 %collective-permute-start = (f32[3,16]{0,1:T(8,128)S(1)}, f32[3,16]{0,1:T(8,128)S(1)}, u32[]{:S(2)}, u32[]{:S(2)}) collective-permute-start(f32[3,16]{0,1:T(8,128)S(1)} %bitcast.583), channel_id=1, source_target_pairs={{30,0},{0,2},{2,4},{4,6},{6,8},{8,10},{10,12},{12,14},{14,16},{16,... | collective-permute-start | bytes 584 | tf_op jit(solution)/shard_map/ppermute | solution.py:20
  76.2 22.1 %all-to-all-start = ((f32[6,16,3]{0,2,1:T(4,128)}), f32[6,16,3]{0,2,1:T(4,128)S(1)}, u32[]{:S(2)}, u32[]{:S(2)}) async-start(f32[6,16,3]{0,2,1:T(4,128)} %copy.230), calls=%async_computation | async-start | bytes 65536 | tf_op jit(solution)/shard_map/all_to_all | solution.py:246
  97.1 4.8 %copy-start.1 = (f32[4,8,256]{2,1,0:T(8,128)S(1)}, f32[4,8,256]{2,1,0:T(8,128)}, u32[]{:S(2)}) copy-start(f32[4,8,256]{2,1,0:T(8,128)} %param.21) | copy-start | bytes 98308
  98.3 22.6 %all-to-all-start.3 = ((f32[7,2,12,8,256]{4,3,2,0,1:T(8,128)}), f32[7,2,12,8,256]{4,3,2,0,1:T(8,128)S(1)}, u32[]{:S(2)}, u32[]{:S(2)}) async-start(f32[7,2,12,8,256]{4,3,2,0,1:T(8,128)} %copy.238), calls=%async_computation.3 | async-start | bytes 2752512 | tf_op jit(solution)/shard_map/all_to_all | solution.py:174
  209.3 12.0 %all-to-all-start.4 = ((f32[6,16,3]{0,2,1:T(4,128)}), f32[6,16,3]{0,2,1:T(4,128)S(1)}, u32[]{:S(2)}, u32[]{:S(2)}) async-start(f32[6,16,3]{0,2,1:T(4,128)} %copy.247), calls=%async_computation.4 | async-start | bytes 65536 | tf_op jit(solution)/shard_map/all_to_all | solution.py:254
  216.0 9.2 %copy-start.5 = (f32[64]{0:T(128)S(1)}, f32[64]{0:T(128)}, u32[]{:S(2)}) copy-start(f32[64]{0:T(128)} %param.16) | copy-start | bytes 772
  216.0 11.1 %copy-start.6 = (f32[3,64]{1,0:T(4,128)S(1)}, f32[3,64]{1,0:T(4,128)}, u32[]{:S(2)}) copy-start(f32[3,64]{1,0:T(4,128)} %param.12) | copy-start | bytes 2308
  216.0 11.1 %copy-start.7 = (s32[16]{0:T(128)S(1)}, s32[16]{0:T(128)}, u32[]{:S(2)}) copy-start(s32[16]{0:T(128)} %param.14) | copy-start | bytes 196
  221.4 20.9 %all-to-all-start.5 = ((f32[7,12,2,8,256]{4,3,1,0,2:T(8,128)}), f32[7,12,2,8,256]{4,3,1,0,2:T(8,128)S(1)}, u32[]{:S(2)}, u32[]{:S(2)}) async-start(f32[7,12,2,8,256]{4,3,1,0,2:T(8,128)} %copy.267), calls=%async_computation.5 | async-start | bytes 2752512 | tf_op jit(solution)/shard_map/all_to_all | solution.py:189
  225.6 1.5 collective-permute-start.1
where the time goes:
time: 248 us; the launch traced here: 244 us
  matrix products  74.8 us (30%)
  waiting for transfers between devices  54.8 us (22%)
  starting transfers between devices  41.4 us (17%)
  other arithmetic  30.3 us (12%)
  blocking collectives  22.3 us (9%)
  local copies, waits for them, and re-layouts  18.1 us (7%)
    dot_general x32, matrix products, line_apply(): return jnp.einsum('kx,cbxn->cbkn', table, field, precision=FULL_PREC)  38.1 us
    ppermute x2, waiting for transfers between devices, shifted(): return lax.ppermute(block, axis, route)  33 us
    all_gather x1, blocking collectives, micro_solve(): full_moduli = lax.all_gather(moduli_slab, 'vox', axis=1, tiled=True)  17.9 us
    all_to_all x1, starting transfers between devices, local(): lax.all_to_all(strain_rows, 'macro', split_axis=1, concat_axis=1, tiled=T...  15.5 us
    all_to_all x1, waiting for transfers between devices, micro_solve(): lax.all_to_all(updated.reshape(7, per_rank, ranks_vox, thickness, VOX_PLA...  14.3 us
    dot_general x4, matrix products, spectral_correction(): jnp.dot(back_imag, sin_plane, precision=FULL_PREC)  9.12 us
    dot_general x4, matrix products, spectral_correction(): imag_plane = -jnp.dot(stress, sin_plane, precision=FULL_PREC)  8.95 us
    dot_general x4, matrix products, spectral_correction(): jnp.dot(back_real, cos_plane, precision=FULL_PREC)  8.75 us
  transfers between devices with their start and end apart: 8, of which 6 were waited for; matrix products, arithmetic and copies ran while one was open for 15% of the time, Pallas kernels for 0%

commit v1 on v0

--- a/solution.py
+++ b/solution.py
@@ -1,3 +1,4 @@
+import functools
 import math
 import jax
 import jax.numpy as jnp
@@ -12,6 +13,17 @@
 LAM_REF = 3.0
 MU_REF = 3.0
 FULL_PREC = lax.Precision.HIGHEST
+
+
+def plate_start(vector, out_dim, where_dim):
+    latest = lax.axis_size("macro")
+    low = jnp.split(vector, latest, axis=out_dim)
+    x_new = jnp.stack(low)
+    piece_out = lax.all_to_all(x_new, "macro", 0, 0)
+    return jnp.concatenate(piece_out, axis=where_dim)
+
+
+raise_turns_on_mesh = functools.partial(plate_start, out_dim=1, where_dim=1)
 
 
 def shifted(block, axis, distance):
@@ -243,7 +255,7 @@
     strain_rows = strain[:, slot_source] * valid_float[None, :]
     received, got_strain, got_valid = (
         lax.all_to_all(outgoing, "macro", split_axis=1, concat_axis=1, tiled=True),
-        lax.all_to_all(strain_rows, "macro", split_axis=1, concat_axis=1, tiled=True),
+        raise_turns_on_mesh(strain_rows),
         lax.all_to_all(valid_float[None, :], "macro", split_axis=1, concat_axis=1, tiled=True),
     )
     recv_index, recv_match = pick_slots(got_valid[0] > 0.5, RECV_AGG)

time: 248 us -> 264 us (1.065)
  local copies, waits for them, and re-layouts: 18.1 us -> 27.1 us
  waiting for transfers between devices: 54.8 us -> 62.4 us
    all_to_all x1, waiting for transfers between devices: 0.01 us -> 40.3 us  [local(): lax.all_to_all(outgoing, 'macro', split_axis=1, concat_axis=1, tiled=True)]
    ppermute x2, waiting for transfers between devices: 33 us -> 1.31 us  [shifted(): return lax.ppermute(block, axis, route)]
    unnamed x18 -> x31, local copies, waits for them, and re-layouts: 0.21 us -> 9.7 us
  transfers between devices with their start and end apart: 8 -> 8, of which waited for: 6 -> 5; matrix products, arithmetic and copies ran while one was open for 15% -> 17% of each run, Pallas kernels for 0% -> 0%
where the time goes in v1:
time: 264 us; the launch traced here: 260 us
  matrix products  74.8 us (28%)
  waiting for transfers between devices  62.4 us (24%)
  starting transfers between devices  40.5 us (15%)
  other arithmetic  30.7 us (12%)
  local copies, waits for them, and re-layouts  27.1 us (10%)
  blocking collectives  22.3 us (8%)
    all_to_all x1, waiting for transfers between devices, local(): lax.all_to_all(outgoing, 'macro', split_axis=1, concat_axis=1, tiled=True)  40.3 us
    dot_general x32, matrix products, line_apply(): return jnp.einsum('kx,cbxn->cbkn', table, field, precision=FULL_PREC)  38 us
    all_gather x1, blocking collectives, micro_solve(): full_moduli = lax.all_gather(moduli_slab, 'vox', axis=1, tiled=True)  17.9 us
    all_to_all x1, waiting for transfers between devices, micro_solve(): lax.all_to_all(updated.reshape(7, per_rank, ranks_vox, thickness, VOX_PLA...  14.3 us
    all_to_all x1, starting transfers between devices, plate_start(): piece_out = lax.all_to_all(x_new, 'macro', 0, 0)  13.8 us
    unnamed x31, local copies, waits for them, and re-layouts  9.7 us
    dot_general x4, matrix products, spectral_correction(): jnp.dot(back_imag, sin_plane, precision=FULL_PREC)  9.12 us
    dot_general x4, matrix products, spectral_correction(): imag_plane = -jnp.dot(stress, sin_plane, precision=FULL_PREC)  8.94 us
  transfers between devices with their start and end apart: 8, of which 5 were waited for; matrix products, arithmetic and copies ran while one was open for 17% of the time, Pallas kernels for 0%

profile of v1, /device:TPU:0, one launch (start us, length us, event | category | flops | bytes accessed | tf_op | source)
XLA Modules:
  0.0 259.7 jit_solution(12803455570756755903)
XLA Ops:
  6.4 7.2 %all-to-all-start.1 = ((f32[1,16,3]{2,0,1:T(1,128)}), f32[1,16,3]{2,0,1:T(1,128)S(1)}, u32[]{:S(2)}, u32[]{:S(2)}) async-start(f32[1,16,3]{2,0,1:T(1,128)} %bitcast.30), calls=%async_computation.1 | async-start | bytes 16384 | tf_op jit(solution)/shard_map/all_to_all | solution.py:259
  15.0 2.8 %gather_fusion.4 = f32[48,7,8,256]{3,2,1,0:T(8,128)S(1)} fusion(f32[7,64,8,256]{3,2,1,0:T(8,128)} %param.20, s32[1024]{0:T(1024)S(1)} %get-tuple-element.240), kind=kCustom, calls=%fused_computation.4 | custom fusion | bytes 5505216 | tf_op jit(solution)/shard_map/gather | solution.py:254
  17.8 1.8 multiply_bitcast_fusion
  20.3 4.2 %compare_select_fusion.3 = (f32[256,1]{0,1:T(1,128)S(1)}, f32[256,1]{0,1:T(1,128)S(1)}) fusion(f32[]{:T(128)} %bitcast.70, f32[]{:T(128)} %bitcast.71, f32[]{:T(128)} %bitcast.72, f32[]{:T(128)} %bitcast.73, f32[]{:T(128)} %bitcast.74, f32[]{:T(128)} %bitcast.76, f32[]{:T(128)} %bitcast.75), kind=kLoop, calls=%fused_computation.522 | loop fusion | flops 10752 | bytes 2076 | tf_op jit(solution)/shard_map/gather | solution.py:155
  24.5 5.5 %broadcast_multiply_fusion = (f32[256]{0:T(256)S(1)}, f32[256]{0:T(256)S(1)}) fusion(pred[256]{0:T(512)(128)(4,1)S(1)} %compare_reduce_fusion.1, pred[256]{0:T(512)(128)(4,1)S(1)} %compare_reduce_fusion.2, pred[256]{0:T(512)(128)(4,1)S(1)} %compare_reduce_fusion.3, pred[256]{0:T(512)(128)(4,1)S(1)} %compare_reduce_fusion.4, ...), kind=kLoop, calls=%fused_computation.591 | loop fusion | flops 2560 | bytes 5412 | tf_op jit(solution)/shard_map/mul | solution.py:126
  30.0 5.5 %broadcast_multiply_fusion.1 = (f32[256]{0:T(256)S(1)}, f32[256]{0:T(256)S(1)}) fusion(pred[256]{0:T(512)(128)(4,1)S(1)} %compare_reduce_fusion.10, pred[256]{0:T(512)(128)(4,1)S(1)} %compare_reduce_fusion.11, pred[256]{0:T(512)(128)(4,1)S(1)} %compare_reduce_fusion.12, pred[256]{0:T(512)(128)(4,1)S(1)} %compare_reduce_fusion.13, ...), kind=kLoop, calls=%fused_computation.592 | loop fusion | flops 2560 | bytes 5412 | tf_op jit(solution)/shard_map/mul | solution.py:125
  35.6 6.0 %all-to-all-start.2 = ((f32[7,48,8,256]{3,2,0,1:T(8,128)}), f32[7,48,8,256]{3,2,0,1:T(8,128)S(1)}, u32[]{:S(2)}, u32[]{:S(2)}) async-start(f32[7,48,8,256]{3,2,0,1:T(8,128)} %multiply_bitcast_fusion), calls=%async_computation.2 | async-start | bytes 5505024 | tf_op jit(solution)/shard_map/all_to_all | solution.py:257
  53.7 40.3 %all-to-all-done.2 = f32[7,48,8,256]{3,2,0,1:T(8,128)S(1)} async-done(((f32[7,48,8,256]{3,2,0,1:T(8,128)}), f32[7,48,8,256]{3,2,0,1:T(8,128)S(1)}, u32[]{:S(2)}, u32[]{:S(2)}) %all-to-all-start.2) | async-done | bytes 2752544 | tf_op jit(solution)/shard_map/all_to_all | solution.py:257
  94.0 13.8 %all-to-all-start = ((f32[16,6,3]{1,2,0:T(4,128)}), f32[16,6,3]{1,2,0:T(4,128)S(1)}, u32[]{:S(2)}, u32[]{:S(2)}) async-start(f32[16,6,3]{1,2,0:T(4,128)} %constant_dynamic-update-slice_fusion), calls=%async_computation | async-start | bytes 65536 | tf_op jit(solution)/shard_map/all_to_all | solution.py:22
  107.9 1.8 copy.340
  109.7 2.4 gather_fusion.5
  112.1 1.2 copy.342
  114.5 3.6 %all-to-all-start.3 = ((f32[7,2,12,8,256]{4,3,2,0,1:T(8,128)}), f32[7,2,12,8,256]{4,3,2,0,1:T(8,128)S(1)}, u32[]{:S(2)}, u32[]{:S(2)}) async-start(f32[7,2,12,8,256]{4,3,2,0,1:T(8,128)} %copy.342), calls=%async_computation.3 | async-start | bytes 2752512 | tf_op jit(solution)/shard_map/all_to_all | solution.py:186
  118.2 17.9 %all_gather.6 = f32[4,16,256]{2,1,0:T(8,128)S(1)} all-gather(f32[4,8,256]{2,1,0:T(8,128)S(1)} %copy-done.1), channel_id=1, replica_groups=mesh['macro'=16,'vox'=2] {'vox'}, dimensions={1}, use_global_device_ids=true | all-gather | bytes 98304 | tf_op jit(solution)/shard_map/all_gather | solution.py:185
  138.2 2.1 fusion.42
  140.3 2.1 convolution_negate_fusion.3
  142.5 1.2 fusion.189
  143.6 1.2 fusion.185
  144.8 1.2 fusion.23
  146.0 1.2 fusion.22
  148.3 1.4 fusion.183
  150.9 1.2 fusion.20
  152.1 1.2 fusion.21
  153.2 2.1 fusion.40
  155.4 2.2 fusion.7
  158.3 2.1 fusion.38
  160.4 2.5 convolution_negate_fusion.2
  163.0 1.2 fusion.181
  164.1 1.2 fusion.177
  165.3 1.2 fusion.19
  166.5 1.2 fusion.18
  171.2 1.2 fusion.16
  172.4 1.2 fusion.17
  173.5 2.3 fusion.36
  175.8 2.2 fusion.5
  178.7 2.1 fusion.34
  180.9 2.1 convolution_negate_fusion.1
  184.2 1.2 fusion.169
  185.4 1.4 fusion.15
  186.8 1.2 fusion.14
  189.1 1.2 fusion.167
  191.5 1.2 fusion.12
  192.6 1.2 fusion.13
  193.8 2.1 fusion.32
  196.0 2.6 fusion.3
  199.3 2.1 fusion.30
  201.4 2.1 convolution_negate_fusion
  203.6 1.2 fusion.165
  204.7 1.2 fusion.161
  205.9 1.2 fusion.11
  207.1 1.2 fusion.10
  209.4 1.4 fusion.159
  212.0 1.2 fusion.8
  213.1 1.2 fusion.9
  214.3 2.1 fusion.28
  216.5 2.2 fusion.1
  219.8 4.4 %all-gather = f32[2,12,6]{1,2,0:T(8,128)S(1)} all-gather(f32[1,12,6]{1,2,0:T(8,128)S(1)} %multiply_bitcast_fusion.3), channel_id=1, replica_groups=mesh['macro'=16,'vox'=2] {'vox'}, dimensions={0}, use_global_device_ids=true | all-gather | bytes 864 | tf_op jit(solution)/shard_map/all_gather | solution.py:200
  225.3 5.4 %all-to-all-start.4 = ((f32[6,16,3]{0,2,1:T(4,128)}), f32[6,16,3]{0,2,1:T(4,128)S(1)}, u32[]{:S(2)}, u32[]{:S(2)}) async-start(f32[6,16,3]{0,2,1:T(4,128)} %copy.351), calls=%async_computation.4 | async-start | bytes 65536 | tf_op jit(solution)/shard_map/all_to_all | solution.py:266
  230.8 1.2 copy.371
  232.1 5.3 %all-to-all-done.4 = f32[6,16,3]{0,2,1:T(4,128)S(1)} async-done(((f32[6,16,3]{0,2,1:T(4,128)}), f32[6,16,3]{0,2,1:T(4,128)S(1)}, u32[]{:S(2)}, u32[]{:S(2)}) %all-to-all-start.4) | async-done | bytes 1184 | tf_op jit(solution)/shard_map/all_to_all | solution.py:266
  237.4 3.6 %all-to-all-start.5 = ((f32[7,12,2,8,256]{4,3,1,0,2:T(8,128)}), f32[7,12,2,8,256]{4,3,1,0,2:T(8,128)S(1)}, u32[]{:S(2)}, u32[]{:S(2)}) async-start(f32[7,12,2,8,256]{4,3,1,0,2:T(8,128)} %copy.371), calls=%async_computation.5 | async-start | bytes 2752512 | tf_op jit(solution)/shard_map/all_to_all | solution.py:201
  241.9 1.3 collective-permute-done.1
  243.9 14.3 %all-to-all-done.5 = f32[7,12,2,8,256]{4,3,1,0,2:T(8,128)S(1)} async-done(((f32[7,12,2,8,256]{4,3,1,0,2:T(8,128)}), f32[7,12,2,8,256]{4,3,1,0,2:T(8,128)S(1)}, u32[]{:S(2)}, u32[]{:S(2)}) %all-to-all-start.5) | async-done | bytes 1376288 | tf_op jit(solution)/shard_map/all_to_all | solution.py:201
  258.3 1.2 copy.361
  (186 shorter events, 40.2 us)
Async XLA Ops:
  5.0 36.7 %collective-permute-start = (f32[3,16]{0,1:T(8,128)S(1)}, f32[3,16]{0,1:T(8,128)S(1)}, u32[]{:S(2)}, u32[]{:S(2)}) collective-permute-start(f32[3,16]{0,1:T(8,128)S(1)} %bitcast.649), channel_id=1, source_target_pairs={{30,0},{0,2},{2,4},{4,6},{6,8},{8,10},{10,12},{12,14},{14,16},{16,... | collective-permute-start | bytes 584 | tf_op jit(solution)/shard_map/ppermute | solution.py:32
  6.4 29.2 %all-to-all-start.1 = ((f32[1,16,3]{2,0,1:T(1,128)}), f32[1,16,3]{2,0,1:T(1,128)S(1)}, u32[]{:S(2)}, u32[]{:S(2)}) async-start(f32[1,16,3]{2,0,1:T(1,128)} %bitcast.30), calls=%async_computation.1 | async-start | bytes 16384 | tf_op jit(solution)/shard_map/all_to_all | solution.py:259
  35.6 7.3 %copy-start = (f32[3,8,64]{2,1,0:T(8,128)S(1)}, f32[3,8,64]{2,1,0:T(8,128)}, u32[]{:S(2)}) copy-start(f32[3,8,64]{2,1,0:T(8,128)} %param.15) | copy-start | bytes 18436
  35.6 7.4 %copy-start.3 = (f32[2,64]{1,0:T(2,128)S(1)}, f32[2,64]{1,0:T(2,128)}, u32[]{:S(2)}) copy-start(f32[2,64]{1,0:T(2,128)} %param.17) | copy-start | bytes 1540
  35.6 58.4 %all-to-all-start.2 = ((f32[7,48,8,256]{3,2,0,1:T(8,128)}), f32[7,48,8,256]{3,2,0,1:T(8,128)S(1)}, u32[]{:S(2)}, u32[]{:S(2)}) async-start(f32[7,48,8,256]{3,2,0,1:T(8,128)} %multiply_bitcast_fusion), calls=%async_computation.2 | async-start | bytes 5505024 | tf_op jit(solution)/shard_map/all_to_all | solution.py:257
  94.0 20.5 %all-to-all-start = ((f32[16,6,3]{1,2,0:T(4,128)}), f32[16,6,3]{1,2,0:T(4,128)S(1)}, u32[]{:S(2)}, u32[]{:S(2)}) async-start(f32[16,6,3]{1,2,0:T(4,128)} %constant_dynamic-update-slice_fusion), calls=%async_computation | async-start | bytes 65536 | tf_op jit(solution)/shard_map/all_to_all | solution.py:22
  113.4 4.8 %copy-start.1 = (f32[4,8,256]{2,1,0:T(8,128)S(1)}, f32[4,8,256]{2,1,0:T(8,128)}, u32[]{:S(2)}) copy-start(f32[4,8,256]{2,1,0:T(8,128)} %param.21) | copy-start | bytes 98308
  114.5 22.6 %all-to-all-start.3 = ((f32[7,2,12,8,256]{4,3,2,0,1:T(8,128)}), f32[7,2,12,8,256]{4,3,2,0,1:T(8,128)S(1)}, u32[]{:S(2)}, u32[]{:S(2)}) async-start(f32[7,2,12,8,256]{4,3,2,0,1:T(8,128)} %copy.342), calls=%async_computation.3 | async-start | bytes 2752512 | tf_op jit(solution)/shard_map/all_to_all | solution.py:186
  225.3 12.1 %all-to-all-start.4 = ((f32[6,16,3]{0,2,1:T(4,128)}), f32[6,16,3]{0,2,1:T(4,128)S(1)}, u32[]{:S(2)}, u32[]{:S(2)}) async-start(f32[6,16,3]{0,2,1:T(4,128)} %copy.351), calls=%async_computation.4 | async-start | bytes 65536 | tf_op jit(solution)/shard_map/all_to_all | solution.py:266
  232.1 9.2 %copy-start.4 = (f32[64]{0:T(128)S(1)}, f32[64]{0:T(128)}, u32[]{:S(2)}) copy-start(f32[64]{0:T(128)} %param.16) | copy-start | bytes 772
  232.1 9.3 %copy-start.2 = (s32[8,64]{1,0:T(8,128)S(1)}, s32[8,64]{1,0:T(8,128)}, u32[]{:S(2)}) copy-start(s32[8,64]{1,0:T(8,128)} %param.13) | copy-start | bytes 6148
  232.1 11.1 %copy-start.5 = (f32[3,64]{1,0:T(4,128)S(1)}, f32[3,64]{1,0:T(4,128)}, u32[]{:S(2)}) copy-start(f32[3,64]{1,0:T(4,128)} %param.12) | copy-start | bytes 2308
  232.1 11.1 %copy-start.6 = (s32[16]{0:T(128)S(1)}, s32[16]{0:T(128)}, u32[]{:S(2)}) copy-start(s32[16]{0:T(128)} %param.14) | copy-start | bytes 196
  237.4 20.9 %all-to-all-start.5 = ((f32[7,12,2,8,256]{4,3,1,0,2:T(8,128)}), f32[7,12,2,8,256]{4,3,1,0,2:T(8,128)S(1)}, u32[]{:S(2)}, u32[]{:S(2)}) async-start(f32[7,12,2,8,256]{4,3,1,0,2:T(8,128)} %copy.371), calls=%async_computation.5 | async-start | bytes 2752512 | tf_op jit(solution)/shard_map/all_to_all | solution.py:201
  241.7 1.5 collective-permute-start.1
